TPU v7x, 32 devices: a whole 2x2x4 slice. The times are simulated.
32 devices in a mesh: long: 16 (over z, y, x), short: 2 (over core).
Axes of the slice: x: 2, y: 2, z: 4, core: 2. Of those that a mesh axis runs over, the one named last changes fastest.
Arguments:
- outer_block: bfloat16 [2, 16, 2, 512, 512], P('short', 'long'), may hold values from -0.15625 to 0.15625
- outflow_block: bfloat16 [2, 16, 2, 512, 512], P('short', 'long'), may hold values from -0.15625 to 0.15625
- inflow_block: bfloat16 [2, 16, 2, 512, 512], P('short', 'long'), may hold values from -0.15625 to 0.15625
- shared_block: bfloat16 [2, 16, 2, 512, 512], P('short', 'long'), may hold values from -1 to 1
Outputs:
- own_block: float32 [2, 2, 512, 4096], P('short', None, None, 'long')
- cross_block: float32 [2, 2, 512, 4096], P('short', None, None, 'long')
All inputs are finite; a program needn't handle non-finite values.
Results may differ from a plain program's by a relative error of at most 0.0095.
Values may be sent and summed in bfloat16 or wider, within the bound.
No kernel may reach another device: no remote copies, remote signals or barrier semaphores. Data moves between devices by JAX's collectives and lax.ppermute only.
A program may use at most 64 MiB of HBM per device.

v0:
```python
import math

import jax
import jax.numpy as jnp
from jax import lax
from jax.sharding import PartitionSpec as P

TERMS = 3


def from_partner(x, axis, bit):
    return lax.ppermute(x, axis, [(i, i ^ 1 << bit) for i in range(lax.axis_size(axis))])


def complex_product(left_matrix, right_matrix):
    upper_rows = jnp.concatenate([left_matrix[0], -left_matrix[1]], axis=1)
    lower_rows = jnp.concatenate([left_matrix[1], left_matrix[0]], axis=1)
    stacked = jnp.concatenate([upper_rows, lower_rows], axis=0)
    column = jnp.concatenate([right_matrix[0], right_matrix[1]], axis=0)
    result = jnp.dot(stacked, column, preferred_element_type=jnp.float32)
    row_count = left_matrix.shape[1]
    return jnp.stack([result[:row_count], result[row_count:]])


def series_of(product, inflow):
    start_value = inflow.astype(jnp.float32)
    current = start_value
    for iteration in range(TERMS - 1):
        current = start_value + complex_product(product, current.astype(jnp.bfloat16))
    return current.astype(jnp.bfloat16)


def shards(outer_block, outflow_block, inflow_block, shared_block):
    outer_self = outer_block[0, 0]
    outflow_self = outflow_block[0, 0]
    inflow_self = inflow_block[0, 0]
    corner_self = shared_block[0, 0]
    received = from_partner(jnp.stack([corner_self, outflow_self]), "long", 0)
    corner_peer = received[0]
    outflow_peer = received[1]
    product = complex_product(corner_self, corner_peer).astype(jnp.bfloat16)
    series = series_of(product, inflow_self)
    mapped = complex_product(corner_peer, series).astype(jnp.bfloat16)
    first_diag = (outer_self.astype(jnp.float32) + complex_product(outflow_self, mapped)).astype(
        jnp.bfloat16
    )
    first_cross = complex_product(outflow_peer, series).astype(jnp.bfloat16)
    parity = lax.axis_index("long") % 2
    left_side = parity == 0
    width = first_diag.shape[1]
    half_width = width // 2
    factor = math.sqrt(width)
    partner_cols = from_partner(jnp.stack([first_diag, first_cross]), "long", 0)
    shared_two = jnp.where(left_side, first_diag, partner_cols[0])
    outflow_two = jnp.where(left_side, first_cross, partner_cols[1])
    inflow_two = jnp.where(left_side, partner_cols[1], first_cross)
    outer_two = jnp.where(left_side, partner_cols[0], first_diag)
    cousin = from_partner(jnp.stack([shared_two, outflow_two]), "short", 0)
    shared_far = cousin[0]
    outflow_far = cousin[1]
    column_start = parity * half_width
    second_product = complex_product(shared_two, shared_far).astype(jnp.bfloat16)
    inflow_part = lax.dynamic_slice_in_dim(inflow_two, column_start, half_width, 2)
    outer_part = lax.dynamic_slice_in_dim(outer_two, column_start, half_width, 2)
    second_series = series_of(second_product, inflow_part)
    second_mapped = complex_product(shared_far, second_series).astype(jnp.bfloat16)
    own_result = factor * (
        outer_part.astype(jnp.float32) + complex_product(outflow_two, second_mapped)
    )
    cross_result = factor * complex_product(outflow_far, second_series)
    return (own_result[None], cross_result[None])


def solution(mesh):
    in_specs = (
        P("short", "long", None, None, None),
        P("short", "long", None, None, None),
        P("short", "long", None, None, None),
        P("short", "long", None, None, None),
    )
    out_specs = (P("short", None, None, "long"), P("short", None, None, "long"))
    return jax.shard_map(shards, mesh=mesh, in_specs=in_specs, out_specs=out_specs, check_vma=False)
```

profile of v0, /device:TPU:1, one launch (start us, length us, event | category | flops | bytes accessed | tf_op | source)
XLA Modules:
  0.0 154.3 jit_solution(15286546814178602809)
XLA Ops:
  0.6 3.1 %pad_maximum_fusion = bf16[2,2,512,512]{3,2,1,0:T(8,128)(2,1)} fusion(bf16[1,2,512,512]{3,2,1,0:T(8,128)(2,1)} %bitcast.143, bf16[1,2,512,512]{3,2,1,0:T(8,128)(2,1)} %bitcast.144), kind=kLoop, calls=%fused_computation.18 | loop fusion | flops 1048576 | bytes 4194304 | tf_op jit(solution)/shard_map/stack | solution.py:38
  3.7 2.0 %collective-permute-start = (bf16[2,2,512,512]{3,2,1,0:T(8,128)(2,1)}, bf16[2,2,512,512]{3,2,1,0:T(8,128)(2,1)}, u32[]{:S(2)}, u32[]{:S(2)}) collective-permute-start(bf16[2,2,512,512]{3,2,1,0:T(8,128)(2,1)} %pad_maximum_fusion), channel_id=1, source_target_pairs={{0,2},{2,0},{4,6},{6,4},{8,10},{10,8},{12,14},{14,12},{16,18},{18,... | collective-permute-start | bytes 6291464 | tf_op jit(solution)/shard_map/ppermute | solution.py:12
  5.7 1.5 copy.6
  7.2 0.9 fusion.131
  8.2 1.0 slice_bitcast_fusion.38
  9.3 0.5 copy-done
  9.8 41.6 %collective-permute-done = bf16[2,2,512,512]{3,2,1,0:T(8,128)(2,1)} collective-permute-done((bf16[2,2,512,512]{3,2,1,0:T(8,128)(2,1)}, bf16[2,2,512,512]{3,2,1,0:T(8,128)(2,1)}, u32[]{:S(2)}, u32[]{:S(2)}) %collective-permute-start) | collective-permute-done | bytes 2097184 | tf_op jit(solution)/shard_map/ppermute | solution.py:12
  51.4 1.7 %slice_bitcast_fusion.33 = (bf16[512,512]{1,0:T(8,128)(2,1)S(1)}, bf16[512,512]{1,0:T(8,128)(2,1)S(1)}, bf16[512,512]{1,0:T(8,128)(2,1)S(1)}, bf16[512,512]{1,0:T(8,128)(2,1)S(1)}) fusion(bf16[2,2,512,512]{3,2,1,0:T(8,128)(2,1)} %collective-permute-done), kind=kLoop, calls=%fused_computation.153 | loop fusion | bytes 4194304 | tf_op jit(solution)/shard_map/squeeze | solution.py:16
  53.1 1.3 fusion.73
  54.5 1.3 fusion.88
  56.0 0.4 fusion.4
  56.5 1.3 fusion.92
  57.9 0.4 fusion.5
  58.5 2.4 %fusion.133 = (bf16[512,512]{1,0:T(8,128)(2,1)}, bf16[512,512]{1,0:T(8,128)(2,1)S(1)}) fusion(bf16[2,2,512,512]{3,2,1,0:T(8,128)(2,1)} %collective-permute-done), kind=kLoop, calls=%fused_computation.189 | loop fusion | flops 524288 | bytes 2097152 | tf_op jit(solution)/shard_map/neg | solution.py:16
  60.9 1.3 fusion.30
  62.3 1.1 fusion.116
  63.4 0.3 copy-done.12
  63.8 5.8 %fusion.6 = f32[1024,512]{0,1:T(8,128)} fusion(bf16[512,512]{1,0:T(8,128)(2,1)} %get-tuple-element.47, bf16[512,512]{1,0:T(8,128)(2,1)S(1)} %copy-done.12, bf16[512,512]{1,0:T(8,128)(2,1)S(1)} %copy-done.11, bf16[512,512]{1,0:T(8,128)(2,1)} %copy-done.17, bf16[512,512]{1,0:T(8,128)(2,1)} %copy-done.18, bf16[512,512]{1,0:T(8,128)(2,1)} %get-tuple-element.21, ...), kind=kOutput, calls=%fused_computation.10 | convolution fusion | flops 2166882304 | bytes 6291456 | tf_op jit(solution)/shard_map/dot_general | solution.py:20
  69.6 3.3 %slice_bitcast_fusion.6 = (f32[1,512,512]{1,2,0:T(8,128)}, f32[1,512,512]{1,2,0:T(8,128)}, f32[1,1,512,512]{2,3,1,0:T(8,128)S(1)}, f32[1,1,512,512]{2,3,1,0:T(8,128)S(1)}) fusion(f32[1024,512]{0,1:T(8,128)} %fusion.6), kind=kLoop, calls=%fused_computation.121 | loop fusion | bytes 6291456 | tf_op jit(solution)/shard_map/stack | solution.py:22
  72.9 0.4 fusion.1
  73.3 0.6 copy-done.1
  73.9 0.4 copy-done.5
  74.3 0.2 copy-done.6
  74.5 1.5 maximum_maximum_fusion.1
  76.0 1.2 collective-permute-start.1
  77.2 45.1 %collective-permute-done.1 = bf16[2,2,512,512]{2,3,1,0:T(8,128)(2,1)} collective-permute-done((bf16[2,2,512,512]{2,3,1,0:T(8,128)(2,1)}, bf16[2,2,512,512]{2,3,1,0:T(8,128)(2,1)}, u32[]{:S(2)}, u32[]{:S(2)}) %collective-permute-start.1) | collective-permute-done | bytes 2097184 | tf_op jit(solution)/shard_map/ppermute | solution.py:12
  122.3 4.4 %slice_bitcast_fusion.9 = (bf16[2,512,512]{1,2,0:T(8,128)(2,1)}, bf16[1,2,512,512]{2,3,1,0:T(8,128)(2,1)S(1)}, bf16[1,2,512,512]{2,3,1,0:T(8,128)(2,1)S(1)}, bf16[2,512,512]{1,2,0:T(8,128)(2,1)}) fusion(bf16[2,2,512,512]{2,3,1,0:T(8,128)(2,1)} %collective-permute-done.1, pred[]{:T(512)S(6)} %eq.5, bf16[1,1,512,512]{2,3,1,0:T(8,128)(2,1)} %get-tuple-element.51, ...), kind=kLoop, calls=%fused_computation.124 | loop fusion | flops 3670016 | bytes 10485761 | tf_op jit(solution)/shard_map/squeeze | solution.py:57
  126.7 1.5 %pad_maximum_fusion.1 = bf16[2,2,512,512]{2,3,1,0:T(8,128)(2,1)} fusion(bf16[1,2,512,512]{2,3,1,0:T(8,128)(2,1)S(1)} %get-tuple-element.14, bf16[1,2,512,512]{2,3,1,0:T(8,128)(2,1)S(1)} %get-tuple-element.13), kind=kLoop, calls=%fused_computation.53 | loop fusion | flops 1048576 | bytes 4194304 | tf_op jit(solution)/shard_map/stack | solution.py:58
  128.2 2.1 %collective-permute-start.2 = (bf16[2,2,512,512]{2,3,1,0:T(8,128)(2,1)}, bf16[2,2,512,512]{2,3,1,0:T(8,128)(2,1)}, u32[]{:S(2)}, u32[]{:S(2)}) collective-permute-start(bf16[2,2,512,512]{2,3,1,0:T(8,128)(2,1)} %pad_maximum_fusion.1), channel_id=1, source_target_pairs={{0,1},{1,0},{2,3},{3,2},{4,5},{5,4},{6,7},{7,6},{8,9},{9,8},{10,11... | collective-permute-start | bytes 6291464 | tf_op jit(solution)/shard_map/ppermute | solution.py:12
  130.5 1.0 copy-done.7
  131.6 0.3 copy-done.8
  131.9 3.4 %broadcast_select_fusion.1 = (bf16[2,512,512]{1,2,0:T(8,128)(2,1)S(1)}, bf16[2,512,512]{1,2,0:T(8,128)(2,1)}, bf16[2,512,512]{1,2,0:T(8,128)(2,1)S(1)}) fusion(pred[]{:T(512)S(6)} %eq.5, bf16[2,2,512,512]{2,3,1,0:T(8,128)(2,1)} %collective-permute-done.1, f32[1,512,512]{1,2,0:T(8,128)S(1)} %copy-done.8, f32[1,512,512]{1,2,0:T(8,128)S(1)} %copy-done.7, ...), kind=kLoop, calls=%fused_computation.118 | loop fusion | flops 3670016 | bytes 9437185 | tf_op jit(solution)/shard_map/jit(_where)/select_n | solution.py:54
  135.3 0.9 fusion.135
  136.2 1.1 slice_bitcast_fusion.20
  137.3 1.7 %slice_bitcast_fusion.12 = (bf16[512,512]{0,1:T(8,128)(2,1)S(1)}, bf16[512,512]{0,1:T(8,128)(2,1)S(1)}, bf16[512,512]{0,1:T(8,128)(2,1)S(1)}, bf16[512,512]{0,1:T(8,128)(2,1)S(1)}) fusion(bf16[2,2,512,512]{2,3,1,0:T(8,128)(2,1)} %collective-permute-done.2), kind=kLoop, calls=%fused_computation.131 | loop fusion | bytes 4194304 | tf_op jit(solution)/shard_map/squeeze | solution.py:16
  139.0 1.4 fusion.70
  140.5 0.7 fusion.105
  141.3 0.2 fusion.83
  141.6 0.7 fusion.106
  142.4 0.2 fusion.84
  142.7 2.2 %fusion.138 = (bf16[512,512]{0,1:T(8,128)(2,1)S(1)}, bf16[512,512]{0,1:T(8,128)(2,1)}) fusion(bf16[2,2,512,512]{2,3,1,0:T(8,128)(2,1)} %collective-permute-done.2), kind=kLoop, calls=%fused_computation.194 | loop fusion | flops 524288 | bytes 2097152 | tf_op jit(solution)/shard_map/neg | solution.py:16
  144.8 0.7 fusion.62
  145.7 4.5 %fusion.38 = f32[1024,256]{0,1:T(8,128)S(1)} fusion(bf16[512,512]{0,1:T(8,128)(2,1)} %get-tuple-element.69, bf16[512,512]{0,1:T(8,128)(2,1)} %get-tuple-element.70, bf16[512,512]{0,1:T(8,128)(2,1)} %get-tuple-element.71, bf16[512,512]{0,1:T(8,128)(2,1)} %copy-done.16, bf16[512,512]{0,1:T(8,128)(2,1)} %copy-done.15, bf16[512,512]{0,1:T(8,128)(2,1)} %get-tuple-element.7, ...), kind=kOutput, calls=%fused_computation.45 | convolution fusion | flops 1091829760 | bytes 4718592 | tf_op jit(solution)/shard_map/dot_general | solution.py:20
  150.3 1.1 copy-done.9
  151.4 0.3 copy-done.10
  151.8 0.2 fusion.100
  152.0 1.3 copy.15
  153.3 1.1 maximum_multiply_fusion
  (49 shorter events, 1.5 us)
Async XLA Ops:
  3.7 3.5 %copy-start.2 = (bf16[1,1,2,512,512]{4,3,2,1,0:T(8,128)(2,1)S(1)}, bf16[1,1,2,512,512]{4,3,2,1,0:T(8,128)(2,1)}, u32[]{:S(2)}) copy-start(bf16[1,1,2,512,512]{4,3,2,1,0:T(8,128)(2,1)} %param.5) | copy-start | bytes 3145732
  3.7 4.4 %copy-start.3 = (bf16[1,1,2,512,512]{4,3,2,1,0:T(8,128)(2,1)S(1)}, bf16[1,1,2,512,512]{4,3,2,1,0:T(8,128)(2,1)}, u32[]{:S(2)}) copy-start(bf16[1,1,2,512,512]{4,3,2,1,0:T(8,128)(2,1)} %param.7) | copy-start | bytes 3145732
  3.7 47.7 %collective-permute-start = (bf16[2,2,512,512]{3,2,1,0:T(8,128)(2,1)}, bf16[2,2,512,512]{3,2,1,0:T(8,128)(2,1)}, u32[]{:S(2)}, u32[]{:S(2)}) collective-permute-start(bf16[2,2,512,512]{3,2,1,0:T(8,128)(2,1)} %pad_maximum_fusion), channel_id=1, source_target_pairs={{0,2},{2,0},{4,6},{6,4},{8,10},{10,8},{12,14},{14,12},{16,18},{18,... | collective-permute-start | bytes 6291464 | tf_op jit(solution)/shard_map/ppermute | solution.py:12
  8.2 1.6 %copy-start = (bf16[1,1,2,512,512]{4,3,2,1,0:T(8,128)(2,1)S(1)}, bf16[1,1,2,512,512]{4,3,2,1,0:T(8,128)(2,1)}, u32[]{:S(2)}) copy-start(bf16[1,1,2,512,512]{4,3,2,1,0:T(8,128)(2,1)} %param.6) | copy-start | bytes 3145732
  53.0 1.3 copy-start.17
  53.0 1.3 copy-start.18
  58.5 3.8 %copy-start.13 = (bf16[512,512]{1,0:T(8,128)(2,1)}, bf16[512,512]{1,0:T(8,128)(2,1)S(1)}, u32[]{:S(2)}) copy-start(bf16[512,512]{1,0:T(8,128)(2,1)S(1)} %get-tuple-element.52) | copy-start | bytes 1572868
  58.5 3.8 %copy-start.14 = (bf16[512,512]{1,0:T(8,128)(2,1)}, bf16[512,512]{1,0:T(8,128)(2,1)S(1)}, u32[]{:S(2)}) copy-start(bf16[512,512]{1,0:T(8,128)(2,1)S(1)} %get-tuple-element.53) | copy-start | bytes 1572868
  62.3 1.2 copy-start.11
  62.3 1.5 copy-start.12
  72.9 1.0 copy-start.1
  72.9 1.4 copy-start.5
  72.9 1.6 %copy-start.6 = (bf16[1,1,512,512]{2,3,1,0:T(8,128)(2,1)S(1)}, bf16[1,1,512,512]{2,3,1,0:T(8,128)(2,1)}, u32[]{:S(2)}) copy-start(bf16[1,1,512,512]{2,3,1,0:T(8,128)(2,1)} %get-tuple-element.51) | copy-start | bytes 1572868
  76.0 46.2 %collective-permute-start.1 = (bf16[2,2,512,512]{2,3,1,0:T(8,128)(2,1)}, bf16[2,2,512,512]{2,3,1,0:T(8,128)(2,1)}, u32[]{:S(2)}, u32[]{:S(2)}) collective-permute-start(bf16[2,2,512,512]{2,3,1,0:T(8,128)(2,1)} %maximum_maximum_fusion.1), channel_id=1, source_target_pairs={{0,2},{2,0},{4,6},{6,4},{8,10},{10,8},{12,14},{14,12},{16,18},{18,... | collective-permute-start | bytes 6291464 | tf_op jit(solution)/shard_map/ppermute | solution.py:12
  126.7 3.7 %copy-start.4 = (bf16[2,512,512]{1,2,0:T(8,128)(2,1)S(1)}, bf16[2,512,512]{1,2,0:T(8,128)(2,1)}, u32[]{:S(2)}) copy-start(bf16[2,512,512]{1,2,0:T(8,128)(2,1)} %get-tuple-element.15) | copy-start | bytes 3145732
  128.2 9.1 %collective-permute-start.2 = (bf16[2,2,512,512]{2,3,1,0:T(8,128)(2,1)}, bf16[2,2,512,512]{2,3,1,0:T(8,128)(2,1)}, u32[]{:S(2)}, u32[]{:S(2)}) collective-permute-start(bf16[2,2,512,512]{2,3,1,0:T(8,128)(2,1)} %pad_maximum_fusion.1), channel_id=1, source_target_pairs={{0,1},{1,0},{2,3},{3,2},{4,5},{5,4},{6,7},{7,6},{8,9},{9,8},{10,11... | collective-permute-start | bytes 6291464 | tf_op jit(solution)/shard_map/ppermute | solution.py:12
  130.3 1.2 copy-start.7
  130.3 1.5 copy-start.8
  139.0 1.4 copy-start.15
  139.0 1.4 copy-start.16
  142.7 2.9 %copy-start.19 = (bf16[512,256]{0,1:T(8,128)(2,1)}, bf16[512,256]{0,1:T(8,128)(2,1)S(1)}, u32[]{:S(2)}) copy-start(bf16[512,256]{0,1:T(8,128)(2,1)S(1)} %get-tuple-element.64) | copy-start | bytes 786436
  150.2 1.2 copy-start.9
  150.2 1.5 copy-start.10
where the time goes:
time: 155 us; the launch traced here: 154 us
  waiting for transfers between devices  86.6 us (56%)
  other arithmetic  23.7 us (15%)
  matrix products  19.1 us (12%)
  local copies, waits for them, and re-layouts  18.6 us (12%)
  starting transfers between devices  5.32 us (3%)
    ppermute x3, waiting for transfers between devices, from_partner(): lax.ppermute(x, axis, [(i, i ^ 1 << bit) for i in range(lax.axis_size(axi...  86.6 us
    dot_general x10, matrix products, complex_product(): result = jnp.dot(stacked, column, preferred_element_type=jnp.float32)  19.1 us
    unnamed x42, local copies, waits for them, and re-layouts  7.67 us
    neg x7, other arithmetic, complex_product(): upper_rows = jnp.concatenate([left_matrix[0], -left_matrix[1]], axis=1)  6.6 us
    squeeze x5, local copies, waits for them, and re-layouts, complex_product(): upper_rows = jnp.concatenate([left_matrix[0], -left_matrix[1]], axis=1)  5.52 us
    ppermute x3, starting transfers between devices, from_partner(): lax.ppermute(x, axis, [(i, i ^ 1 << bit) for i in range(lax.axis_size(axi...  5.32 us
    another operation x8, local copies, waits for them, and re-layouts, complex_product(): return jnp.stack([result[:row_count], result[row_count:]])  5.12 us
    squeeze x1, other arithmetic, shards(): outer_two = jnp.where(left_side, partner_cols[0], first_diag)  4.41 us
  transfers between devices with their start and end apart: 3, of which 2 were waited for; matrix products, arithmetic and copies ran while one was open for 6% of the time, Pallas kernels for 0%

commit v1 on v0

v1 whole, which is shorter than its diff:
```python
import math

import jax
import jax.numpy as jnp
from jax import lax
from jax.sharding import PartitionSpec as P

TERMS = 3


def across(x, axis, parity):
    return lax.ppermute(x, axis, [(i, i ^ 1) for i in range(lax.axis_size(axis)) if i % 2 == parity])


def swap(x, axis):
    return lax.ppermute(x, axis, [(i, i ^ 1) for i in range(lax.axis_size(axis))])


def cdot(left, right):
    upper = jnp.concatenate([left[0], -left[1]], axis=1)
    lower = jnp.concatenate([left[1], left[0]], axis=1)
    stacked = jnp.concatenate([upper, lower], axis=0)
    column = jnp.concatenate([right[0], right[1]], axis=0)
    result = jnp.dot(stacked, column, preferred_element_type=jnp.float32)
    rows = left.shape[1]
    return jnp.stack([result[:rows], result[rows:]])


def rb(x):
    return x.astype(jnp.bfloat16)


def wide(x):
    return x.astype(jnp.float32)


def shards(outer_block, outflow_block, inflow_block, shared_block):
    outer, outflow, inflow, shared = outer_block[0, 0], outflow_block[0, 0], inflow_block[0, 0], shared_block[0, 0]
    width = outer.shape[2]
    half = width // 2
    is_left = lax.axis_index("long") % 2 == 0
    factor = math.sqrt(width)

    shared_r = across(shared, "long", 1)
    inflow_r1 = across(inflow[:, :, half:], "long", 1)
    inflow_r0 = across(inflow[:, :, :half], "long", 1)
    outflow_r = across(outflow, "long", 1)
    outer_r0 = across(outer[:, :, :half], "long", 1)

    product = rb(cdot(shared, shared_r))
    start = wide(inflow)
    series = rb(start + cdot(product, rb(start + cdot(product, inflow))))
    mapped = rb(cdot(shared_r, series))
    diag = rb(wide(outer) + cdot(outflow, mapped))
    diag_far = swap(diag, "short")
    series_far = swap(series, "short")
    product_two = rb(cdot(diag, diag_far))

    def columns(g):
        k = cdot(shared, g)
        kb = rb(k)
        v1 = rb(k + cdot(product, kb))
        shared_series = k + cdot(product, v1)
        right_series = rb(wide(g) + cdot(shared_r, v1))
        cross = rb(cdot(outflow, right_series))
        start_two = wide(cross)
        w = rb(start_two + cdot(product_two, rb(start_two + cdot(product_two, cross))))
        z = rb(cdot(diag_far, w))
        return rb(shared_series + cdot(series, z)), rb(cdot(series_far, w))

    x1, y1 = columns(inflow_r1)
    x1_r = across(x1, "long", 0)
    y1_r = across(y1, "long", 0)
    x0, y0 = columns(inflow_r0)

    outflow_b = jnp.where(is_left, outflow_r, outflow)
    outflow_b_far = swap(outflow_b, "short")
    x = jnp.where(is_left, x0, x1_r)
    y = jnp.where(is_left, y0, y1_r)
    outer_b = jnp.where(is_left, outer_r0, outer[:, :, half:])
    own = factor * (wide(outer_b) + cdot(outflow_b, x))
    far = factor * cdot(outflow_b_far, y)
    return own[None], far[None]


def solution(mesh):
    spec = P("short", "long", None, None, None)
    out = P("short", None, None, "long")
    return jax.shard_map(shards, mesh=mesh, in_specs=(spec,) * 4, out_specs=(out, out), check_vma=False)
```

time: 155 us -> 136 us (0.88)
  waiting for transfers between devices: 86.6 us -> 34.6 us
  matrix products: 19.1 us -> 34.4 us
  local copies, waits for them, and re-layouts: 18.6 us -> 30.9 us
  starting transfers between devices: 5.32 us -> 14.1 us
  other arithmetic: 23.7 us -> 18.2 us
    ppermute x3 -> x10, waiting for transfers between devices: 86.6 us -> 34.6 us  [the longest x7 34.6 us: across(): lax.ppermute(x, axis, [(i, i ^ 1) for i in range(lax.axis_size(axis)) if...]
    dot_general x10 -> x25, matrix products: 19.1 us -> 34.4 us  [cdot(): result = jnp.dot(stacked, column, preferred_element_type=jnp.float32)]
    ppermute x3 -> x10, starting transfers between devices: 5.32 us -> 14.1 us  [the longest x7 10.7 us: across(): lax.ppermute(x, axis, [(i, i ^ 1) for i in range(lax.axis_size(axis)) if...]
    squeeze x11 -> x25, local copies, waits for them, and re-layouts: 5.84 us -> 12.2 us  [the longest x8 8.03 us: cdot(): upper = jnp.concatenate([left[0], -left[1]], axis=1)]
    another operation x3 -> x1, other arithmetic: 6.16 us -> 0.87 us  [cdot(): return jnp.stack([result[:rows], result[rows:]])]
    squeeze x1 -> x0, other arithmetic: 4.41 us -> none  [shards(): outer_two = jnp.where(left_side, partner_cols[0], first_diag)]
    slice x0 -> x2, local copies, waits for them, and re-layouts: none -> 3.16 us  [the longest x1 2.32 us: shards(): inflow_r0 = across(inflow[:, :, :half], 'long', 1)]
    another operation x8 -> x23, local copies, waits for them, and re-layouts: 5.12 us -> 7.35 us  [cdot(): return jnp.stack([result[:rows], result[rows:]])]
  transfers between devices with their start and end apart: 3 -> 10, of which waited for: 2 -> 2; matrix products, arithmetic and copies ran while one was open for 6% -> 53% of each run, Pallas kernels for 0% -> 0%
where the time goes in v1:
time: 136 us; the launch traced here: 134 us
  waiting for transfers between devices  34.6 us (25%)
  matrix products  34.4 us (25%)
  local copies, waits for them, and re-layouts  30.9 us (23%)
  other arithmetic  18.2 us (13%)
  starting transfers between devices  14.1 us (10%)
  between operations  1.7 us (1%)
    ppermute x7, waiting for transfers between devices, across(): lax.ppermute(x, axis, [(i, i ^ 1) for i in range(lax.axis_size(axis)) if...  34.6 us
    dot_general x25, matrix products, cdot(): result = jnp.dot(stacked, column, preferred_element_type=jnp.float32)  34.4 us
    ppermute x7, starting transfers between devices, across(): lax.ppermute(x, axis, [(i, i ^ 1) for i in range(lax.axis_size(axis)) if...  10.7 us
    neg x11, other arithmetic, cdot(): upper = jnp.concatenate([left[0], -left[1]], axis=1)  8.35 us
    unnamed x108, local copies, waits for them, and re-layouts  8.22 us
    squeeze x8, local copies, waits for them, and re-layouts, cdot(): upper = jnp.concatenate([left[0], -left[1]], axis=1)  8.03 us
    another operation x23, local copies, waits for them, and re-layouts, cdot(): return jnp.stack([result[:rows], result[rows:]])  7.35 us
    squeeze x17, local copies, waits for them, and re-layouts, cdot(): column = jnp.concatenate([right[0], right[1]], axis=0)  4.13 us
  transfers between devices with their start and end apart: 10, of which 2 were waited for; matrix products, arithmetic and copies ran while one was open for 53% of the time, Pallas kernels for 0%

profile of v1, /device:TPU:1, one launch (start us, length us, event | category | flops | bytes accessed | tf_op | source)
XLA Modules:
  0.0 133.9 jit_solution(13258100362392906683)
XLA Ops:
  0.6 2.3 %fusion.146 = (bf16[2,512,256]{2,1,0:T(8,128)(2,1)}, bf16[2,512,256]{2,1,0:T(8,128)(2,1)}) fusion(bf16[2,512,512]{2,1,0:T(8,128)(2,1)} %bitcast.222), kind=kLoop, calls=%fused_computation.280 | loop fusion | bytes 2097152 | tf_op jit(solution)/shard_map/slice | solution.py:46
  3.0 1.3 collective-permute-start.2
  4.3 1.3 collective-permute-start.3
  5.6 1.3 collective-permute-start.5
  6.9 1.3 collective-permute-start.1
  8.2 0.8 slice.587
  9.0 1.3 collective-permute-start
  10.3 2.1 %slice_bitcast_fusion.58 = (bf16[512,512]{1,0:T(8,128)(2,1)S(1)}, bf16[512,512]{1,0:T(8,128)(2,1)}) fusion(bf16[1,1,2,512,512]{4,3,2,1,0:T(8,128)(2,1)} %param.7), kind=kLoop, calls=%fused_computation.202 | loop fusion | bytes 2097152 | tf_op jit(solution)/shard_map/squeeze | solution.py:20
  12.4 1.3 fusion.135
  13.7 2.1 %fusion.136 = bf16[512,512]{1,0:T(8,128)(2,1)} fusion(bf16[1,1,2,512,512]{4,3,2,1,0:T(8,128)(2,1)} %param.5), kind=kLoop, calls=%fused_computation.268 | loop fusion | flops 262144 | bytes 1048576 | tf_op jit(solution)/shard_map/neg | solution.py:20
  15.8 2.3 %slice_bitcast_fusion.54 = (bf16[512,512]{1,0:T(8,128)(2,1)}, bf16[512,512]{1,0:T(8,128)(2,1)}) fusion(bf16[1,1,2,512,512]{4,3,2,1,0:T(8,128)(2,1)} %param.5), kind=kLoop, calls=%fused_computation.198 | loop fusion | bytes 2097152 | tf_op jit(solution)/shard_map/squeeze | solution.py:20
  18.3 1.0 copy-done.42
  20.1 31.8 %collective-permute-done.5 = bf16[2,512,256]{2,1,0:T(8,128)(2,1)S(1)} collective-permute-done((bf16[2,512,256]{2,1,0:T(8,128)(2,1)}, bf16[2,512,256]{2,1,0:T(8,128)(2,1)S(1)}, u32[]{:S(2)}, u32[]{:S(2)}) %collective-permute-start.5) | collective-permute-done | bytes 524320 | tf_op jit(solution)/shard_map/ppermute | solution.py:12
  52.9 0.9 slice_bitcast_fusion.93
  54.5 1.3 slice_bitcast_fusion.49
  55.8 0.8 copy-done.36
  56.6 1.3 convolution_convert_fusion.1
  58.0 1.3 fusion.42
  60.0 1.3 fusion.46
  61.8 1.0 copy-done.1
  62.8 1.1 slice_bitcast_fusion.41
  63.9 1.1 fusion.138
  65.0 6.0 %fusion.64 = f32[1024,512]{1,0:T(8,128)} fusion(bf16[512,512]{1,0:T(8,128)(2,1)} %get-tuple-element.50, bf16[512,512]{1,0:T(8,128)(2,1)} %get-tuple-element.49, bf16[512,512]{1,0:T(8,128)(2,1)} %copy-done.36, bf16[512,512]{1,0:T(8,128)(2,1)} %copy-done.38, bf16[512,512]{1,0:T(8,128)(2,1)S(1)} %fusion.138, bf16[512,512]{1,0:T(8,128)(2,1)} %get-tuple-element.48, ...), kind=kOutput, calls=%fused_computation.101 | convolution fusion | flops 2166882304 | bytes 6291456 | tf_op jit(solution)/shard_map/dot_general | solution.py:24
  70.9 1.8 %slice_bitcast_fusion.1 = (f32[1,512,512]{2,1,0:T(8,128)S(1)}, f32[1,512,512]{2,1,0:T(8,128)S(1)}) fusion(f32[1024,512]{1,0:T(8,128)} %fusion.64), kind=kLoop, calls=%fused_computation.58 | loop fusion | bytes 4194304 | tf_op jit(solution)/shard_map/stack | solution.py:26
  73.2 2.1 %collective-permute-start.4 = (bf16[2,512,512]{2,1,0:T(8,128)(2,1)S(1)}, bf16[2,512,512]{2,1,0:T(8,128)(2,1)S(1)}, u32[]{:S(2)}, u32[]{:S(2)}) collective-permute-start(bf16[2,512,512]{2,1,0:T(8,128)(2,1)S(1)} %fusion.10), channel_id=1, source_target_pairs={{0,1},{1,0},{2,3},{3,2},{4,5},{5,4},{6,7},{7,6},{8,9},{9,8},{10,11... | collective-permute-start | bytes 3145736 | tf_op jit(solution)/shard_map/ppermute | solution.py:16
  77.2 0.8 fusion.139
  79.6 1.7 %broadcast_select_fusion = bf16[2,512,512]{2,1,0:T(8,128)(2,1)S(1)} fusion(bf16[2,512,512]{2,1,0:T(8,128)(2,1)} %collective-permute-done.1, pred[]{:T(512)S(6)} %eq.5, bf16[1,1,2,512,512]{4,3,2,1,0:T(8,128)(2,1)} %param.5), kind=kLoop, calls=%fused_computation.100 | loop fusion | flops 524288 | bytes 3145729 | tf_op jit(solution)/shard_map/jit(_where)/select_n | solution.py:76
  81.9 1.0 slice_bitcast_fusion.52
  83.0 0.8 fusion.137
  84.8 0.9 fusion.88
  87.7 0.9 copy-done.11
  90.7 1.0 slice_bitcast_fusion.45
  92.5 1.0 slice_bitcast_fusion.23
  93.6 1.3 fusion.27
  101.4 0.9 pad_maximum_fusion.8
  102.3 2.1 %collective-permute-start.9 = (bf16[2,512,256]{2,1,0:T(8,128)(2,1)}, bf16[2,512,256]{2,1,0:T(8,128)(2,1)}, u32[]{:S(2)}, u32[]{:S(2)}) collective-permute-start(bf16[2,512,256]{2,1,0:T(8,128)(2,1)} %pad_maximum_fusion.8), channel_id=1, source_target_pairs={{0,2},{4,6},{8,10},{12,14},{16,18},{20,22},{24,26},{28,30},{1,3},{... | collective-permute-start | bytes 1572872 | tf_op jit(solution)/shard_map/ppermute | solution.py:12
  104.4 0.8 fusion.140
  105.3 5.5 %fusion.31 = f32[1024,256]{1,0:T(8,128)} fusion(bf16[512,512]{1,0:T(8,128)(2,1)} %copy-done.35, bf16[512,512]{1,0:T(8,128)(2,1)} %copy-done.34, bf16[512,512]{1,0:T(8,128)(2,1)} %fusion.140, bf16[512,512]{1,0:T(8,128)(2,1)} %get-tuple-element.49, bf16[512,512]{1,0:T(8,128)(2,1)} %get-tuple-element.50, bf16[512,512]{1,0:T(8,128)(2,1)} %fusion.139, ...), kind=kOutput, calls=%fused_computation.52 | convolution fusion | flops 1091829760 | bytes 4718592 | tf_op jit(solution)/shard_map/dot_general | solution.py:24
  110.8 1.4 %slice_bitcast_fusion.15 = (f32[1,512,256]{2,1,0:T(8,128)S(1)}, f32[1,512,256]{2,1,0:T(8,128)S(1)}) fusion(f32[1024,256]{1,0:T(8,128)} %fusion.31), kind=kLoop, calls=%fused_computation.114 | loop fusion | bytes 2097152 | tf_op jit(solution)/shard_map/stack | solution.py:26
  112.3 1.0 fusion.59
  113.3 2.1 %collective-permute-start.6 = (bf16[2,512,256]{2,1,0:T(8,128)(2,1)}, bf16[2,512,256]{2,1,0:T(8,128)(2,1)}, u32[]{:S(2)}, u32[]{:S(2)}) collective-permute-start(bf16[2,512,256]{2,1,0:T(8,128)(2,1)} %fusion.59), channel_id=1, source_target_pairs={{0,2},{4,6},{8,10},{12,14},{16,18},{20,22},{24,26},{28,30},{1,3},{... | collective-permute-start | bytes 1572872 | tf_op jit(solution)/shard_map/ppermute | solution.py:12
  116.8 4.5 %fusion.30 = f32[1024,256]{1,0:T(8,128)S(1)} fusion(bf16[512,512]{1,0:T(8,128)(2,1)} %copy-done.35, bf16[512,512]{1,0:T(8,128)(2,1)} %copy-done.34, bf16[512,512]{1,0:T(8,128)(2,1)} %fusion.140, bf16[512,512]{1,0:T(8,128)(2,1)} %get-tuple-element.49, bf16[512,512]{1,0:T(8,128)(2,1)} %get-tuple-element.50, bf16[512,512]{1,0:T(8,128)(2,1)} %fusion.139, ...), kind=kOutput, calls=%fused_computation.51 | convolution fusion | flops 1091829760 | bytes 4718592 | tf_op jit(solution)/shard_map/dot_general | solution.py:24
  121.3 1.1 fusion.142
  122.5 1.4 %slice_bitcast_fusion.10 = (bf16[512,512]{1,0:T(8,128)(2,1)S(1)}, bf16[512,512]{1,0:T(8,128)(2,1)S(1)}) fusion(bf16[2,512,512]{2,1,0:T(8,128)(2,1)} %collective-permute-done.7), kind=kLoop, calls=%fused_computation.109 | loop fusion | bytes 2097152 | tf_op jit(solution)/shard_map/squeeze | solution.py:20
  123.9 2.7 %collective-permute-done.6 = bf16[2,512,256]{2,1,0:T(8,128)(2,1)} collective-permute-done((bf16[2,512,256]{2,1,0:T(8,128)(2,1)}, bf16[2,512,256]{2,1,0:T(8,128)(2,1)}, u32[]{:S(2)}, u32[]{:S(2)}) %collective-permute-start.6) | collective-permute-done | bytes 524320 | tf_op jit(solution)/shard_map/ppermute | solution.py:12
  128.1 1.1 maximum_multiply_fusion
  130.6 1.1 copy-done.5
  131.7 2.2 %fusion.62 = f32[1,2,512,256]{3,2,1,0:T(8,128)} fusion(f32[1,512,256]{2,1,0:T(8,128)S(1)} %get-tuple-element.15, f32[1,512,256]{2,1,0:T(8,128)S(1)} %get-tuple-element.14, bf16[2,512,256]{2,1,0:T(8,128)(2,1)} %collective-permute-done, bf16[2,512,512]{2,1,0:T(8,128)(2,1)S(1)} %bitcast.224, pred[]{:T(512)S(6)} %eq.5), kind=kLoop, calls=%fused_computation.98 | loop fusion | flops 1310720 | bytes 3145729 | tf_op jit(solution)/shard_map/broadcast_in_dim | solution.py:83
  (185 shorter events, 24.8 us)
Async XLA Ops:
  0.6 7.5 %copy-start.3 = (bf16[1,1,2,512,512]{4,3,2,1,0:T(8,128)(2,1)S(1)}, bf16[1,1,2,512,512]{4,3,2,1,0:T(8,128)(2,1)}, u32[]{:S(2)}) copy-start(bf16[1,1,2,512,512]{4,3,2,1,0:T(8,128)(2,1)} %param.4) | copy-start | bytes 3145732
  3.0 15.2 %collective-permute-start.2 = (bf16[2,512,256]{2,1,0:T(8,128)(2,1)}, bf16[2,512,256]{2,1,0:T(8,128)(2,1)S(1)}, u32[]{:S(2)}, u32[]{:S(2)}) collective-permute-start(bf16[2,512,256]{2,1,0:T(8,128)(2,1)} %get-tuple-element.30), channel_id=1, source_target_pairs={{2,0},{6,4},{10,8},{14,12},{18,16},{22,20},{26,24},{30,28},{3,1},{... | collective-permute-start | bytes 1572872 | tf_op jit(solution)/shard_map/ppermute | solution.py:12
  4.3 50.3 %collective-permute-start.3 = (bf16[2,512,512]{2,1,0:T(8,128)(2,1)}, bf16[2,512,512]{2,1,0:T(8,128)(2,1)}, u32[]{:S(2)}, u32[]{:S(2)}) collective-permute-start(bf16[2,512,512]{2,1,0:T(8,128)(2,1)} %bitcast.11), channel_id=1, source_target_pairs={{2,0},{6,4},{10,8},{14,12},{18,16},{22,20},{26,24},{30,28},{3,1},{... | collective-permute-start | bytes 3145736 | tf_op jit(solution)/shard_map/ppermute | solution.py:12
  5.6 46.3 %collective-permute-start.5 = (bf16[2,512,256]{2,1,0:T(8,128)(2,1)}, bf16[2,512,256]{2,1,0:T(8,128)(2,1)S(1)}, u32[]{:S(2)}, u32[]{:S(2)}) collective-permute-start(bf16[2,512,256]{2,1,0:T(8,128)(2,1)} %get-tuple-element.31), channel_id=1, source_target_pairs={{2,0},{6,4},{10,8},{14,12},{18,16},{22,20},{26,24},{30,28},{3,1},{... | collective-permute-start | bytes 1572872 | tf_op jit(solution)/shard_map/ppermute | solution.py:12
  6.9 72.8 %collective-permute-start.1 = (bf16[2,512,512]{2,1,0:T(8,128)(2,1)}, bf16[2,512,512]{2,1,0:T(8,128)(2,1)}, u32[]{:S(2)}, u32[]{:S(2)}) collective-permute-start(bf16[2,512,512]{2,1,0:T(8,128)(2,1)} %bitcast.1), channel_id=1, source_target_pairs={{2,0},{6,4},{10,8},{14,12},{18,16},{22,20},{26,24},{30,28},{3,1},{... | collective-permute-start | bytes 3145736 | tf_op jit(solution)/shard_map/ppermute | solution.py:12
  9.0 121.6 %collective-permute-start = (bf16[2,512,256]{2,1,0:T(8,128)(2,1)}, bf16[2,512,256]{2,1,0:T(8,128)(2,1)}, u32[]{:S(2)}, u32[]{:S(2)}) collective-permute-start(bf16[2,512,256]{2,1,0:T(8,128)(2,1)} %slice.587), channel_id=1, source_target_pairs={{2,0},{6,4},{10,8},{14,12},{18,16},{22,20},{26,24},{30,28},{3,1},{... | collective-permute-start | bytes 1572872 | tf_op jit(solution)/shard_map/ppermute | solution.py:12
  12.3 5.9 %copy-start.40 = (bf16[512,512]{1,0:T(8,128)(2,1)}, bf16[512,512]{1,0:T(8,128)(2,1)S(1)}, u32[]{:S(2)}) copy-start(bf16[512,512]{1,0:T(8,128)(2,1)S(1)} %get-tuple-element.66) | copy-start | bytes 1572868
  12.4 5.7 %copy-start = (bf16[1,1,2,512,512]{4,3,2,1,0:T(8,128)(2,1)S(1)}, bf16[1,1,2,512,512]{4,3,2,1,0:T(8,128)(2,1)}, u32[]{:S(2)}) copy-start(bf16[1,1,2,512,512]{4,3,2,1,0:T(8,128)(2,1)} %param.6) | copy-start | bytes 3145732
  13.7 4.6 %copy-start.24 = (bf16[512,512]{1,0:T(8,128)(2,1)}, bf16[512,512]{1,0:T(8,128)(2,1)S(1)}, u32[]{:S(2)}) copy-start(bf16[512,512]{1,0:T(8,128)(2,1)S(1)} %fusion.135) | copy-start | bytes 1572868
  18.2 1.8 %copy-start.12 = (bf16[2,512,256]{2,1,0:T(8,128)(2,1)}, bf16[2,512,256]{2,1,0:T(8,128)(2,1)S(1)}, u32[]{:S(2)}) copy-start(bf16[2,512,256]{2,1,0:T(8,128)(2,1)S(1)} %collective-permute-done.2) | copy-start | bytes 1572868
  20.0 32.0 %copy-start.25 = (bf16[512,512]{1,0:T(8,128)(2,1)S(1)}, bf16[512,512]{1,0:T(8,128)(2,1)}, u32[]{:S(2)}) copy-start(bf16[512,512]{1,0:T(8,128)(2,1)} %copy-done.24) | copy-start | bytes 1572868
  20.0 32.0 %copy-start.41 = (bf16[512,512]{1,0:T(8,128)(2,1)S(1)}, bf16[512,512]{1,0:T(8,128)(2,1)}, u32[]{:S(2)}) copy-start(bf16[512,512]{1,0:T(8,128)(2,1)} %copy-done.40) | copy-start | bytes 1572868
  55.8 2.1 %copy-start.38 = (bf16[512,512]{1,0:T(8,128)(2,1)}, bf16[512,512]{1,0:T(8,128)(2,1)S(1)}, u32[]{:S(2)}) copy-start(bf16[512,512]{1,0:T(8,128)(2,1)S(1)} %get-tuple-element.63) | copy-start | bytes 1572868
  58.0 1.9 %copy-start.15 = (bf16[512,512]{0,1:T(8,128)(2,1)}, bf16[512,512]{0,1:T(8,128)(2,1)S(1)}, u32[]{:S(2)}) copy-start(bf16[512,512]{0,1:T(8,128)(2,1)S(1)} %get-tuple-element.59) | copy-start | bytes 1572868
  58.0 1.9 %copy-start.17 = (bf16[512,512]{0,1:T(8,128)(2,1)}, bf16[512,512]{0,1:T(8,128)(2,1)S(1)}, u32[]{:S(2)}) copy-start(bf16[512,512]{0,1:T(8,128)(2,1)S(1)} %get-tuple-element.60) | copy-start | bytes 1572868
  58.0 1.9 %copy-start.19 = (bf16[512,512]{0,1:T(8,128)(2,1)}, bf16[512,512]{0,1:T(8,128)(2,1)S(1)}, u32[]{:S(2)}) copy-start(bf16[512,512]{0,1:T(8,128)(2,1)S(1)} %get-tuple-element.61) | copy-start | bytes 1572868
  62.8 2.1 %copy-start.22 = (bf16[512,512]{1,0:T(8,128)(2,1)S(1)}, bf16[512,512]{1,0:T(8,128)(2,1)}, u32[]{:S(2)}) copy-start(bf16[512,512]{1,0:T(8,128)(2,1)} %fusion.136) | copy-start | bytes 1572868
  64.9 13.0 %copy-start.26 = (bf16[512,512]{1,0:T(8,128)(2,1)}, bf16[512,512]{1,0:T(8,128)(2,1)S(1)}, u32[]{:S(2)}) copy-start(bf16[512,512]{1,0:T(8,128)(2,1)S(1)} %fusion.138) | copy-start | bytes 1572868
  70.9 1.9 %copy-start.4 = (bf16[1,1,2,512,512]{4,3,2,1,0:T(8,128)(2,1)S(1)}, bf16[1,1,2,512,512]{4,3,2,1,0:T(8,128)(2,1)}, u32[]{:S(2)}) copy-start(bf16[1,1,2,512,512]{4,3,2,1,0:T(8,128)(2,1)} %param.4) | copy-start | bytes 3145732
  72.8 2.5 %copy-start.2 = (bf16[2,512,512]{2,1,0:T(8,128)(2,1)S(1)}, bf16[2,512,512]{2,1,0:T(8,128)(2,1)}, u32[]{:S(2)}) copy-start(bf16[2,512,512]{2,1,0:T(8,128)(2,1)} %copy-done.1) | copy-start | bytes 3145732
  72.8 3.2 %copy-start.16 = (bf16[512,512]{0,1:T(8,128)(2,1)S(1)}, bf16[512,512]{0,1:T(8,128)(2,1)}, u32[]{:S(2)}) copy-start(bf16[512,512]{0,1:T(8,128)(2,1)} %copy-done.15) | copy-start | bytes 1572868
  72.8 3.2 %copy-start.18 = (bf16[512,512]{0,1:T(8,128)(2,1)S(1)}, bf16[512,512]{0,1:T(8,128)(2,1)}, u32[]{:S(2)}) copy-start(bf16[512,512]{0,1:T(8,128)(2,1)} %copy-done.17) | copy-start | bytes 1572868
  72.8 3.2 %copy-start.20 = (bf16[512,512]{0,1:T(8,128)(2,1)S(1)}, bf16[512,512]{0,1:T(8,128)(2,1)}, u32[]{:S(2)}) copy-start(bf16[512,512]{0,1:T(8,128)(2,1)} %copy-done.19) | copy-start | bytes 1572868
  72.8 3.2 %copy-start.48 = (bf16[512,256]{1,0:T(8,128)(2,1)S(1)}, bf16[512,256]{1,0:T(8,128)(2,1)}, u32[]{:S(2)}) copy-start(bf16[512,256]{1,0:T(8,128)(2,1)} %get-tuple-element.88) | copy-start | bytes 786436
  72.8 3.2 %copy-start.49 = (bf16[512,256]{1,0:T(8,128)(2,1)S(1)}, bf16[512,256]{1,0:T(8,128)(2,1)}, u32[]{:S(2)}) copy-start(bf16[512,256]{1,0:T(8,128)(2,1)} %get-tuple-element.89) | copy-start | bytes 786436
  73.2 20.4 %collective-permute-start.4 = (bf16[2,512,512]{2,1,0:T(8,128)(2,1)S(1)}, bf16[2,512,512]{2,1,0:T(8,128)(2,1)S(1)}, u32[]{:S(2)}, u32[]{:S(2)}) collective-permute-start(bf16[2,512,512]{2,1,0:T(8,128)(2,1)S(1)} %fusion.10), channel_id=1, source_target_pairs={{0,1},{1,0},{2,3},{3,2},{4,5},{5,4},{6,7},{7,6},{8,9},{9,8},{10,11... | collective-permute-start | bytes 3145736 | tf_op jit(solution)/shard_map/ppermute | solution.py:16
  75.3 24.6 %collective-permute-start.8 = (bf16[2,512,512]{2,1,0:T(8,128)(2,1)S(1)}, bf16[2,512,512]{2,1,0:T(8,128)(2,1)S(1)}, u32[]{:S(2)}, u32[]{:S(2)}) collective-permute-start(bf16[2,512,512]{2,1,0:T(8,128)(2,1)S(1)} %copy-done.2), channel_id=1, source_target_pairs={{0,1},{1,0},{2,3},{3,2},{4,5},{5,4},{6,7},{7,6},{8,9},{9,8},{10,11... | collective-permute-start | bytes 3145736 | tf_op jit(solution)/shard_map/ppermute | solution.py:16
  81.3 40.1 %collective-permute-start.7 = (bf16[2,512,512]{2,1,0:T(8,128)(2,1)S(1)}, bf16[2,512,512]{2,1,0:T(8,128)(2,1)}, u32[]{:S(2)}, u32[]{:S(2)}) collective-permute-start(bf16[2,512,512]{2,1,0:T(8,128)(2,1)S(1)} %broadcast_select_fusion), channel_id=1, source_target_pairs={{0,1},{1,0},{2,3},{3,2},{4,5},{5,4},{6,7},{7,6},{8,9},{9,8},{10,11... | collective-permute-start | bytes 3145736 | tf_op jit(solution)/shard_map/ppermute | solution.py:16
  82.9 1.2 copy-start.13
  87.7 1.3 copy-start.32
  87.7 1.4 %copy-start.33 = (bf16[512,512]{1,0:T(8,128)(2,1)S(1)}, bf16[512,512]{1,0:T(8,128)(2,1)}, u32[]{:S(2)}) copy-start(bf16[512,512]{1,0:T(8,128)(2,1)} %get-tuple-element.48) | copy-start | bytes 1572868
  93.6 1.3 %copy-start.34 = (bf16[512,512]{1,0:T(8,128)(2,1)}, bf16[512,512]{1,0:T(8,128)(2,1)S(1)}, u32[]{:S(2)}) copy-start(bf16[512,512]{1,0:T(8,128)(2,1)S(1)} %get-tuple-element.45) | copy-start | bytes 1572868
  93.6 1.3 %copy-start.35 = (bf16[512,512]{1,0:T(8,128)(2,1)}, bf16[512,512]{1,0:T(8,128)(2,1)S(1)}, u32[]{:S(2)}) copy-start(bf16[512,512]{1,0:T(8,128)(2,1)S(1)} %get-tuple-element.46) | copy-start | bytes 1572868
  99.9 15.5 %copy-start.50 = (bf16[512,256]{1,0:T(8,128)(2,1)}, bf16[512,256]{1,0:T(8,128)(2,1)S(1)}, u32[]{:S(2)}) copy-start(bf16[512,256]{1,0:T(8,128)(2,1)S(1)} %get-tuple-element.78) | copy-start | bytes 786436
  100.1 1.3 copy-start.28
  102.3 21.6 %collective-permute-start.9 = (bf16[2,512,256]{2,1,0:T(8,128)(2,1)}, bf16[2,512,256]{2,1,0:T(8,128)(2,1)}, u32[]{:S(2)}, u32[]{:S(2)}) collective-permute-start(bf16[2,512,256]{2,1,0:T(8,128)(2,1)} %pad_maximum_fusion.8), channel_id=1, source_target_pairs={{0,2},{4,6},{8,10},{12,14},{16,18},{20,22},{24,26},{28,30},{1,3},{... | collective-permute-start | bytes 1572872 | tf_op jit(solution)/shard_map/ppermute | solution.py:12
  110.8 1.4 %copy-start.8 = (f32[1,512,256]{2,1,0:T(8,128)S(1)}, f32[1,512,256]{2,1,0:T(8,128)}, u32[]{:S(2)}) copy-start(f32[1,512,256]{2,1,0:T(8,128)} %get-tuple-element.55) | copy-start | bytes 1572868
  110.8 1.5 %copy-start.9 = (f32[1,512,256]{2,1,0:T(8,128)S(1)}, f32[1,512,256]{2,1,0:T(8,128)}, u32[]{:S(2)}) copy-start(f32[1,512,256]{2,1,0:T(8,128)} %get-tuple-element.56) | copy-start | bytes 1572868
  112.1 3.2 %copy-start.29 = (bf16[512,512]{1,0:T(8,128)(2,1)S(1)}, bf16[512,512]{1,0:T(8,128)(2,1)}, u32[]{:S(2)}) copy-start(bf16[512,512]{1,0:T(8,128)(2,1)} %copy-done.28) | copy-start | bytes 1572868
  112.1 3.2 %copy-start.44 = (bf16[512,512]{1,0:T(8,128)(2,1)S(1)}, bf16[512,512]{1,0:T(8,128)(2,1)}, u32[]{:S(2)}) copy-start(bf16[512,512]{1,0:T(8,128)(2,1)} %copy-done.43) | copy-start | bytes 1572868
  112.1 3.2 %copy-start.46 = (bf16[512,512]{1,0:T(8,128)(2,1)S(1)}, bf16[512,512]{1,0:T(8,128)(2,1)}, u32[]{:S(2)}) copy-start(bf16[512,512]{1,0:T(8,128)(2,1)} %copy-done.45) | copy-start | bytes 1572868
  112.2 3.2 %copy-start.51 = (bf16[512,256]{1,0:T(8,128)(2,1)S(1)}, bf16[512,256]{1,0:T(8,128)(2,1)}, u32[]{:S(2)}) copy-start(bf16[512,256]{1,0:T(8,128)(2,1)} %get-tuple-element.79) | copy-start | bytes 786436
  113.3 13.4 %collective-permute-start.6 = (bf16[2,512,256]{2,1,0:T(8,128)(2,1)}, bf16[2,512,256]{2,1,0:T(8,128)(2,1)}, u32[]{:S(2)}, u32[]{:S(2)}) collective-permute-start(bf16[2,512,256]{2,1,0:T(8,128)(2,1)} %fusion.59), channel_id=1, source_target_pairs={{0,2},{4,6},{8,10},{12,14},{16,18},{20,22},{24,26},{28,30},{1,3},{... | collective-permute-start | bytes 1572872 | tf_op jit(solution)/shard_map/ppermute | solution.py:12
  122.4 4.2 %copy-start.6 = (f32[1,512,256]{2,1,0:T(8,128)S(1)}, f32[1,512,256]{2,1,0:T(8,128)}, u32[]{:S(2)}) copy-start(f32[1,512,256]{2,1,0:T(8,128)} %get-tuple-element.16) | copy-start | bytes 1572868
  122.4 4.2 %copy-start.7 = (f32[1,512,256]{2,1,0:T(8,128)S(1)}, f32[1,512,256]{2,1,0:T(8,128)}, u32[]{:S(2)}) copy-start(f32[1,512,256]{2,1,0:T(8,128)} %get-tuple-element.17) | copy-start | bytes 1572868
  122.4 4.2 %copy-start.14 = (bf16[1,512,256]{2,1,0:T(8,128)(2,1)S(1)}, bf16[1,512,256]{2,1,0:T(8,128)(2,1)}, u32[]{:S(2)}) copy-start(bf16[1,512,256]{2,1,0:T(8,128)(2,1)} %get-tuple-element.73) | copy-start | bytes 786436
  128.0 1.5 %copy-start.30 = (bf16[512,512]{1,0:T(8,128)(2,1)S(1)}, bf16[512,512]{1,0:T(8,128)(2,1)}, u32[]{:S(2)}) copy-start(bf16[512,512]{1,0:T(8,128)(2,1)} %get-tuple-element.68) | copy-start | bytes 1572868
  128.0 1.7 %copy-start.31 = (bf16[512,512]{1,0:T(8,128)(2,1)S(1)}, bf16[512,512]{1,0:T(8,128)(2,1)}, u32[]{:S(2)}) copy-start(bf16[512,512]{1,0:T(8,128)(2,1)} %get-tuple-element.69) | copy-start | bytes 1572868
  (16 other events, 16.5 us)

commit v2 on v1

v2 whole, which is shorter than its diff:
```python
import functools
import math

import jax
import jax.numpy as jnp
from jax import lax
from jax.experimental import pallas as pl
from jax.experimental.pallas import tpu as pltpu
from jax.sharding import PartitionSpec as P


BF = jnp.bfloat16
F32 = jnp.float32


def across(x, axis, parity):
    return lax.ppermute(x, axis, [(i, i ^ 1) for i in range(lax.axis_size(axis)) if i % 2 == parity])


def swap(x, axis):
    return lax.ppermute(x, axis, [(i, i ^ 1) for i in range(lax.axis_size(axis))])


def cstage(left, right, emit, rows=256):
    n, k = left.shape[1], left.shape[2]
    m = right.shape[2]

    def body(i, carry):
        r = pl.ds(pl.multiple_of(i * rows, rows), rows)
        re, im = left[0, r, :], left[1, r, :]
        top = jnp.concatenate([re, -im], axis=1)
        bottom = jnp.concatenate([im, re], axis=1)
        lhs = jnp.concatenate([top, bottom], axis=0)
        out = jnp.dot(lhs, right[...].reshape(2 * k, m), preferred_element_type=F32)
        emit(r, out[:rows], out[rows:])
        return carry

    lax.fori_loop(0, n // rows, body, 0)


def plain(dst):
    def emit(r, re, im):
        dst[0, r, :] = re.astype(dst.dtype)
        dst[1, r, :] = im.astype(dst.dtype)

    return emit


def plus(dst, base):
    def emit(r, re, im):
        dst[0, r, :] = (base[0, r, :].astype(F32) + re).astype(dst.dtype)
        dst[1, r, :] = (base[1, r, :].astype(F32) + im).astype(dst.dtype)

    return emit


def level_one(t, h, hr, g, f, e, p, s, d, v, m):
    cstage(h, hr, plain(p))
    cstage(p, g, plus(v, g))
    cstage(p, v, plus(s, g))
    cstage(hr, s, plain(m))
    cstage(f, m, plus(d, e))


def gate(x, t):
    t[...] = x[...]


def second_product(d, df, q):
    cstage(d, df, plain(q))


def columns(h, hr, p, f, g, q, df, s, sf, xy, k32, kb, v1, sb, c, w1, w, z):
    def emit_k(r, re, im):
        k32[0, r, :] = re
        k32[1, r, :] = im
        kb[0, r, :] = re.astype(BF)
        kb[1, r, :] = im.astype(BF)

    cstage(h, g, emit_k)
    cstage(p, kb, plus(v1, k32))
    cstage(hr, v1, plus(sb, g))
    cstage(p, v1, plus(k32, k32))
    cstage(f, sb, plain(c))
    cstage(q, c, plus(w1, c))
    cstage(q, w1, plus(w, c))
    cstage(df, w, plain(z))
    cstage(s, z, plus(xy.at[0], k32))
    cstage(sf, w, plain(xy.at[1]))


def last(factor, f, ff, xy, own, far):
    def scaled(dst):
        def emit(r, re, im):
            dst[0, r, :] = re * factor
            dst[1, r, :] = im * factor

        return emit

    cstage(f, xy.at[0], scaled(own))
    cstage(ff, xy.at[1], scaled(far))


def call(body, outs, args, units, scratch=()):
    n = args[-1].shape[1]
    return pl.pallas_call(
        body,
        out_shape=[jax.ShapeDtypeStruct(s, t) for s, t in outs],
        in_specs=[pl.BlockSpec(memory_space=pltpu.VMEM)] * len(args),
        out_specs=[pl.BlockSpec(memory_space=pltpu.VMEM)] * len(outs),
        scratch_shapes=[pltpu.VMEM(s, t) for s, t in scratch],
        cost_estimate=pl.CostEstimate(
            flops=int(8 * n * n * n * units), bytes_accessed=4 * n * n * (len(args) + len(outs)), transcendentals=0
        ),
    )(*args)


def shards(outer_block, outflow_block, inflow_block, shared_block):
    outer, outflow, inflow, shared = outer_block[0, 0], outflow_block[0, 0], inflow_block[0, 0], shared_block[0, 0]
    n = outer.shape[2]
    half = n // 2
    is_left = lax.axis_index("long") % 2 == 0
    factor = math.sqrt(n)
    full, part = (2, n, n), (2, n, half)

    shared_r = across(shared, "long", 1)
    inflow_r1 = across(inflow[:, :, half:], "long", 1)
    inflow_r0 = across(inflow[:, :, :half], "long", 1)
    outflow_r = across(outflow, "long", 1)
    outer_r0 = across(outer[:, :, :half], "long", 1)

    token = pl.pallas_call(
        gate,
        grid=(1,),
        out_shape=jax.ShapeDtypeStruct((1, 16, 128), BF),
        in_specs=[pl.BlockSpec((1, 16, 128), lambda i: (0, 0, 0))],
        out_specs=pl.BlockSpec((1, 16, 128), lambda i: (0, 0, 0)),
        name="gate",
    )(outer)
    product, series, diag = call(
        level_one, [(full, BF)] * 3, (token, shared, shared_r, inflow, outflow, outer), 5, [(full, BF)] * 2
    )
    diag_far = swap(diag, "short")
    series_far = swap(series, "short")
    (product_two,) = call(second_product, [(full, BF)], (diag, diag_far), 1)

    def half_columns(g):
        return call(
            columns,
            [((2,) + part, BF)],
            (shared, shared_r, product, outflow, g, product_two, diag_far, series, series_far),
            5,
            [(part, F32)] + [(part, BF)] * 7,
        )[0]

    xy1 = half_columns(inflow_r1)
    xy1_r = across(xy1, "long", 0)
    xy0 = half_columns(inflow_r0)

    outflow_b = jnp.where(is_left, outflow_r, outflow)
    outflow_b_far = swap(outflow_b, "short")
    xy = jnp.where(is_left, xy0, xy1_r)
    own, far = call(functools.partial(last, factor), [(part, F32)] * 2, (outflow_b, outflow_b_far, xy), 1)
    outer_b = jnp.where(is_left, outer_r0, outer[:, :, half:])
    own = own + factor * outer_b.astype(F32)
    return own[None], far[None]


def solution(mesh):
    spec = P("short", "long", None, None, None)
    out = P("short", None, None, "long")
    return jax.shard_map(shards, mesh=mesh, in_specs=(spec,) * 4, out_specs=(out, out), check_vma=False)
```

time: 136 us -> 128 us (0.941)
  the two profiles are of different devices: /device:TPU:1 before, /device:TPU:26 now
where the time goes in v2:
time: 128 us; the launch traced here: 127 us
  waiting for transfers between devices  50.1 us (39%)
  Pallas kernels  47.4 us (37%)
  starting transfers between devices  18.6 us (15%)
  other arithmetic  6.08 us (5%)
  local copies, waits for them, and re-layouts  4.6 us (4%)
    ppermute x6, waiting for transfers between devices, across(): lax.ppermute(x, axis, [(i, i ^ 1) for i in range(lax.axis_size(axis)) if...  50.1 us
    pallas_call x5, Pallas kernels, call(): pl.pallas_call(body, out_shape=[jax.ShapeDtypeStruct(s, t) for s, t in ou...  46.1 us
    ppermute x6, starting transfers between devices, across(): lax.ppermute(x, axis, [(i, i ^ 1) for i in range(lax.axis_size(axis)) if...  18 us
    unnamed x12, local copies, waits for them, and re-layouts  2.77 us
  transfers between devices with their start and end apart: 9, of which 3 were waited for; matrix products, arithmetic and copies ran while one was open for 4% of the time, Pallas kernels for 29%

profile of v2, /device:TPU:26, one launch (start us, length us, event | category | flops | bytes accessed | tf_op | source)
XLA Modules:
  0.0 127.5 jit_solution(7129073826215663028)
XLA Ops:
  0.6 2.5 %collective-permute-start.2 = (bf16[2,512,512]{2,1,0:T(8,128)(2,1)}, bf16[2,512,512]{2,1,0:T(8,128)(2,1)S(1)}, u32[]{:S(2)}, u32[]{:S(2)}) collective-permute-start(bf16[2,512,512]{2,1,0:T(8,128)(2,1)} %bitcast.14), channel_id=1, source_target_pairs={{2,0},{6,4},{10,8},{14,12},{18,16},{22,20},{26,24},{30,28},{3,1},{... | collective-permute-start | bytes 3145736 | tf_op jit(solution)/shard_map/ppermute | solution.py:17
  3.1 1.3 %gate.1.t = bf16[1,16,128]{2,1,0:T(8,128)(2,1)} custom-call(bf16[2,512,512]{2,1,0:T(8,128)(2,1)} %bitcast.8), custom_call_target="tpu_custom_call" | custom-call | tf_op jit(solution)/shard_map/gate/pallas_call | solution.py:132
  4.4 21.4 %collective-permute-done.2.hr = bf16[2,512,512]{2,1,0:T(8,128)(2,1)S(1)} collective-permute-done((bf16[2,512,512]{2,1,0:T(8,128)(2,1)}, bf16[2,512,512]{2,1,0:T(8,128)(2,1)S(1)}, u32[]{:S(2)}, u32[]{:S(2)}) %collective-permute-start.2) | collective-permute-done | bytes 1048608 | tf_op jit(solution)/shard_map/ppermute | solution.py:17
  25.8 0.0 copy-start.4
  25.8 1.0 copy-done.4
  26.8 0.0 copy-start.3
  26.8 10.7 %shard_map.59 = (bf16[2,512,512]{2,1,0:T(8,128)(2,1)}, bf16[2,512,512]{2,1,0:T(8,128)(2,1)}, bf16[2,512,512]{2,1,0:T(8,128)(2,1)}) custom-call(bf16[1,16,128]{2,1,0:T(8,128)(2,1)} %gate.1.t, bf16[2,512,512]{2,1,0:T(8,128)(2,1)} %bitcast.15, bf16[2,512,512]{2,1,0:T(8,128)(2,1)} %copy-done.4, bf16[2,512,512]{2,1,0:T(8,128)(2,1)} %bitcast.12, ...), custom_call_target="tpu_custom_call" | custom-call | flops 5368709120 | bytes 9437184 | tf_op jit(solution)/shard_map/pallas_call | solution.py:106
  37.4 0.0 collective-permute-start.4
  37.5 0.5 collective-permute-start.5
  38.0 4.3 %collective-permute-start = (bf16[2,512,512]{2,1,0:T(8,128)(2,1)}, bf16[2,512,512]{2,1,0:T(8,128)(2,1)S(1)}, u32[]{:S(2)}, u32[]{:S(2)}) collective-permute-start(bf16[2,512,512]{2,1,0:T(8,128)(2,1)} %bitcast.f), channel_id=1, source_target_pairs={{2,0},{6,4},{10,8},{14,12},{18,16},{22,20},{26,24},{30,28},{3,1},{... | collective-permute-start | bytes 3145736 | tf_op jit(solution)/shard_map/ppermute | solution.py:17
  42.3 0.0 copy-done.3
  42.3 0.9 fusion
  43.2 1.3 %collective-permute-start.6 = (bf16[2,512,256]{2,1,0:T(8,128)(2,1)S(1)}, bf16[2,512,256]{2,1,0:T(8,128)(2,1)S(1)}, u32[]{:S(2)}, u32[]{:S(2)}) collective-permute-start(bf16[2,512,256]{2,1,0:T(8,128)(2,1)S(1)} %get-tuple-element.12), channel_id=1, source_target_pairs={{2,0},{6,4},{10,8},{14,12},{18,16},{22,20},{26,24},{30,28},{3,1},{... | collective-permute-start | bytes 1572872 | tf_op jit(solution)/shard_map/ppermute | solution.py:17
  44.5 2.1 %collective-permute-start.3 = (bf16[2,512,256]{2,1,0:T(8,128)(2,1)}, bf16[2,512,256]{2,1,0:T(8,128)(2,1)}, u32[]{:S(2)}, u32[]{:S(2)}) collective-permute-start(bf16[2,512,256]{2,1,0:T(8,128)(2,1)} %get-tuple-element.13), channel_id=1, source_target_pairs={{2,0},{6,4},{10,8},{14,12},{18,16},{22,20},{26,24},{30,28},{3,1},{... | collective-permute-start | bytes 1572872 | tf_op jit(solution)/shard_map/ppermute | solution.py:17
  46.6 0.0 collective-permute-done.4.df
  46.6 4.0 %shard_map.60.q = bf16[2,512,512]{2,1,0:T(8,128)(2,1)} custom-call(bf16[2,512,512]{2,1,0:T(8,128)(2,1)} %get-tuple-element.8.d, bf16[2,512,512]{2,1,0:T(8,128)(2,1)} %collective-permute-done.4.df), custom_call_target="tpu_custom_call" | custom-call | flops 1073741824 | bytes 3145728 | tf_op jit(solution)/shard_map/pallas_call | solution.py:106
  50.6 26.6 %collective-permute-done.6.g = bf16[2,512,256]{2,1,0:T(8,128)(2,1)S(1)} collective-permute-done((bf16[2,512,256]{2,1,0:T(8,128)(2,1)S(1)}, bf16[2,512,256]{2,1,0:T(8,128)(2,1)S(1)}, u32[]{:S(2)}, u32[]{:S(2)}) %collective-permute-start.6) | collective-permute-done | bytes 524320 | tf_op jit(solution)/shard_map/ppermute | solution.py:17
  77.2 0.0 copy-start.5
  77.2 0.0 collective-permute-done.5.sf
  77.2 0.8 copy-done.5
  78.0 13.4 %shard_map.62 = bf16[2,2,512,256]{3,2,1,0:T(8,128)(2,1)} custom-call(bf16[2,512,512]{2,1,0:T(8,128)(2,1)} %bitcast.16, bf16[2,512,512]{2,1,0:T(8,128)(2,1)} %copy-done.4, bf16[2,512,512]{2,1,0:T(8,128)(2,1)} %get-tuple-element.7.p, bf16[2,512,512]{2,1,0:T(8,128)(2,1)} %bitcast.f, bf16[2,512,256]{2,1,0:T(8,128)(2,1)} %copy-done.5, ...), custom_call_target="tpu_custom_call" | custom-call | flops 5368709120 | bytes 10485760 | tf_op jit(solution)/shard_map/pallas_call | solution.py:106
  91.4 0.0 copy-start.1
  91.4 1.4 %collective-permute-start.7 = (bf16[2,2,512,256]{3,2,1,0:T(8,128)(2,1)}, bf16[2,2,512,256]{3,2,1,0:T(8,128)(2,1)}, u32[]{:S(2)}, u32[]{:S(2)}) collective-permute-start(bf16[2,2,512,256]{3,2,1,0:T(8,128)(2,1)} %shard_map.62), channel_id=1, source_target_pairs={{0,2},{4,6},{8,10},{12,14},{16,18},{20,22},{24,26},{28,30},{1,3},{... | collective-permute-start | bytes 3145736 | tf_op jit(solution)/shard_map/ppermute | solution.py:17
  92.8 0.0 collective-permute-done
  92.8 1.3 %broadcast_select_fusion.1.f = bf16[2,512,512]{2,1,0:T(8,128)(2,1)S(1)} fusion(bf16[2,512,512]{2,1,0:T(8,128)(2,1)S(1)} %collective-permute-done, pred[]{:T(512)S(6)} %eq.5, bf16[1,1,2,512,512]{4,3,2,1,0:T(8,128)(2,1)} %param.5), kind=kLoop, calls=%fused_computation.2 | loop fusion | flops 524288 | bytes 3145729 | tf_op jit(solution)/shard_map/jit(_where)/select_n | solution.py:160
  94.2 0.0 copy-start
  94.2 0.1 collective-permute-start.1
  94.3 0.0 copy-done.1
  94.3 1.0 slice.18
  95.3 6.3 %collective-permute-start.8 = (bf16[2,512,256]{2,1,0:T(8,128)(2,1)}, bf16[2,512,256]{2,1,0:T(8,128)(2,1)}, u32[]{:S(2)}, u32[]{:S(2)}) collective-permute-start(bf16[2,512,256]{2,1,0:T(8,128)(2,1)} %slice.18), channel_id=1, source_target_pairs={{2,0},{6,4},{10,8},{14,12},{18,16},{22,20},{26,24},{30,28},{3,1},{... | collective-permute-start | bytes 1572872 | tf_op jit(solution)/shard_map/ppermute | solution.py:17
  101.6 0.0 collective-permute-done.3.g
  101.6 13.4 %shard_map.61 = bf16[2,2,512,256]{3,2,1,0:T(8,128)(2,1)} custom-call(bf16[2,512,512]{2,1,0:T(8,128)(2,1)} %bitcast.17, bf16[2,512,512]{2,1,0:T(8,128)(2,1)} %copy-done.4, bf16[2,512,512]{2,1,0:T(8,128)(2,1)} %get-tuple-element.7.p, bf16[2,512,512]{2,1,0:T(8,128)(2,1)} %bitcast.f, bf16[2,512,256]{2,1,0:T(8,128)(2,1)} %collective-permute-done.3.g, ...), custom_call_target="tpu_custom_call" | custom-call | flops 5368709120 | bytes 10485760 | tf_op jit(solution)/shard_map/pallas_call | solution.py:106
  115.0 0.0 copy-done
  115.0 2.1 %collective-permute-done.7 = bf16[2,2,512,256]{3,2,1,0:T(8,128)(2,1)} collective-permute-done((bf16[2,2,512,256]{3,2,1,0:T(8,128)(2,1)}, bf16[2,2,512,256]{3,2,1,0:T(8,128)(2,1)}, u32[]{:S(2)}, u32[]{:S(2)}) %collective-permute-start.7) | collective-permute-done | bytes 1048608 | tf_op jit(solution)/shard_map/ppermute | solution.py:17
  117.1 2.4 %broadcast_select_fusion.xy = bf16[2,2,512,256]{3,2,1,0:T(8,128)(2,1)} fusion(bf16[2,2,512,256]{3,2,1,0:T(8,128)(2,1)} %shard_map.61, bf16[2,2,512,256]{3,2,1,0:T(8,128)(2,1)} %collective-permute-done.7, pred[]{:T(512)S(6)} %eq.5), kind=kLoop, calls=%fused_computation.1 | loop fusion | flops 524288 | bytes 3145729 | tf_op jit(solution)/shard_map/jit(_where)/select_n | solution.py:162
  119.5 0.0 collective-permute-done.1.ff
  119.5 0.0 copy-start.2
  119.5 1.0 copy-done.2
  120.5 4.6 %shard_map.63 = (f32[2,512,256]{2,1,0:T(8,128)}, f32[2,512,256]{2,1,0:T(8,128)}) custom-call(bf16[2,512,512]{2,1,0:T(8,128)(2,1)} %copy-done, bf16[2,512,512]{2,1,0:T(8,128)(2,1)} %copy-done.2, bf16[2,2,512,256]{3,2,1,0:T(8,128)(2,1)} %broadcast_select_fusion.xy), custom_call_target="tpu_custom_call" | custom-call | flops 64 | bytes 80 | tf_op jit(solution)/shard_map/pallas_call | solution.py:106
  125.1 0.0 collective-permute-done.8
  125.1 2.4 %add_bitcast_fusion = f32[1,2,512,256]{3,2,1,0:T(8,128)} fusion(f32[2,512,256]{2,1,0:T(8,128)} %get-tuple-element.10, bf16[2,512,256]{2,1,0:T(8,128)(2,1)} %collective-permute-done.8, bf16[2,512,512]{2,1,0:T(8,128)(2,1)S(1)} %bitcast.11, pred[]{:T(512)S(6)} %eq.5), kind=kLoop, calls=%fused_computation | loop fusion | flops 1048576 | bytes 3145729 | tf_op jit(solution)/shard_map/broadcast_in_dim | solution.py:166
Async XLA Ops:
  0.6 25.2 %collective-permute-start.2 = (bf16[2,512,512]{2,1,0:T(8,128)(2,1)}, bf16[2,512,512]{2,1,0:T(8,128)(2,1)S(1)}, u32[]{:S(2)}, u32[]{:S(2)}) collective-permute-start(bf16[2,512,512]{2,1,0:T(8,128)(2,1)} %bitcast.14), channel_id=1, source_target_pairs={{2,0},{6,4},{10,8},{14,12},{18,16},{22,20},{26,24},{30,28},{3,1},{... | collective-permute-start | bytes 3145736 | tf_op jit(solution)/shard_map/ppermute | solution.py:17
  25.8 1.0 copy-start.4
  26.8 15.5 %copy-start.3 = (bf16[1,1,2,512,512]{4,3,2,1,0:T(8,128)(2,1)S(1)}, bf16[1,1,2,512,512]{4,3,2,1,0:T(8,128)(2,1)}, u32[]{:S(2)}) copy-start(bf16[1,1,2,512,512]{4,3,2,1,0:T(8,128)(2,1)} %param.6) | copy-start | bytes 3145732
  37.4 9.2 %collective-permute-start.4 = (bf16[2,512,512]{2,1,0:T(8,128)(2,1)}, bf16[2,512,512]{2,1,0:T(8,128)(2,1)}, u32[]{:S(2)}, u32[]{:S(2)}) collective-permute-start(bf16[2,512,512]{2,1,0:T(8,128)(2,1)} %get-tuple-element.8.d), channel_id=1, source_target_pairs={{0,1},{1,0},{2,3},{3,2},{4,5},{5,4},{6,7},{7,6},{8,9},{9,8},{10,11... | collective-permute-start | bytes 3145736 | tf_op jit(solution)/shard_map/ppermute | solution.py:21
  37.5 39.8 %collective-permute-start.5 = (bf16[2,512,512]{2,1,0:T(8,128)(2,1)}, bf16[2,512,512]{2,1,0:T(8,128)(2,1)}, u32[]{:S(2)}, u32[]{:S(2)}) collective-permute-start(bf16[2,512,512]{2,1,0:T(8,128)(2,1)} %get-tuple-element.9.s), channel_id=1, source_target_pairs={{0,1},{1,0},{2,3},{3,2},{4,5},{5,4},{6,7},{7,6},{8,9},{9,8},{10,11... | collective-permute-start | bytes 3145736 | tf_op jit(solution)/shard_map/ppermute | solution.py:21
  38.0 54.9 %collective-permute-start = (bf16[2,512,512]{2,1,0:T(8,128)(2,1)}, bf16[2,512,512]{2,1,0:T(8,128)(2,1)S(1)}, u32[]{:S(2)}, u32[]{:S(2)}) collective-permute-start(bf16[2,512,512]{2,1,0:T(8,128)(2,1)} %bitcast.f), channel_id=1, source_target_pairs={{2,0},{6,4},{10,8},{14,12},{18,16},{22,20},{26,24},{30,28},{3,1},{... | collective-permute-start | bytes 3145736 | tf_op jit(solution)/shard_map/ppermute | solution.py:17
  43.2 34.0 %collective-permute-start.6 = (bf16[2,512,256]{2,1,0:T(8,128)(2,1)S(1)}, bf16[2,512,256]{2,1,0:T(8,128)(2,1)S(1)}, u32[]{:S(2)}, u32[]{:S(2)}) collective-permute-start(bf16[2,512,256]{2,1,0:T(8,128)(2,1)S(1)} %get-tuple-element.12), channel_id=1, source_target_pairs={{2,0},{6,4},{10,8},{14,12},{18,16},{22,20},{26,24},{30,28},{3,1},{... | collective-permute-start | bytes 1572872 | tf_op jit(solution)/shard_map/ppermute | solution.py:17
  44.5 57.1 %collective-permute-start.3 = (bf16[2,512,256]{2,1,0:T(8,128)(2,1)}, bf16[2,512,256]{2,1,0:T(8,128)(2,1)}, u32[]{:S(2)}, u32[]{:S(2)}) collective-permute-start(bf16[2,512,256]{2,1,0:T(8,128)(2,1)} %get-tuple-element.13), channel_id=1, source_target_pairs={{2,0},{6,4},{10,8},{14,12},{18,16},{22,20},{26,24},{30,28},{3,1},{... | collective-permute-start | bytes 1572872 | tf_op jit(solution)/shard_map/ppermute | solution.py:17
  77.2 0.8 copy-start.5
  91.4 2.9 %copy-start.1 = (bf16[1,1,2,512,512]{4,3,2,1,0:T(8,128)(2,1)S(1)}, bf16[1,1,2,512,512]{4,3,2,1,0:T(8,128)(2,1)}, u32[]{:S(2)}) copy-start(bf16[1,1,2,512,512]{4,3,2,1,0:T(8,128)(2,1)} %param.4) | copy-start | bytes 3145732
  91.4 25.7 %collective-permute-start.7 = (bf16[2,2,512,256]{3,2,1,0:T(8,128)(2,1)}, bf16[2,2,512,256]{3,2,1,0:T(8,128)(2,1)}, u32[]{:S(2)}, u32[]{:S(2)}) collective-permute-start(bf16[2,2,512,256]{3,2,1,0:T(8,128)(2,1)} %shard_map.62), channel_id=1, source_target_pairs={{0,2},{4,6},{8,10},{12,14},{16,18},{20,22},{24,26},{28,30},{1,3},{... | collective-permute-start | bytes 3145736 | tf_op jit(solution)/shard_map/ppermute | solution.py:17
  94.2 20.8 %copy-start = (bf16[2,512,512]{2,1,0:T(8,128)(2,1)}, bf16[2,512,512]{2,1,0:T(8,128)(2,1)S(1)}, u32[]{:S(2)}) copy-start(bf16[2,512,512]{2,1,0:T(8,128)(2,1)S(1)} %broadcast_select_fusion.1.f) | copy-start | bytes 3145732
  94.2 25.3 %collective-permute-start.1 = (bf16[2,512,512]{2,1,0:T(8,128)(2,1)S(1)}, bf16[2,512,512]{2,1,0:T(8,128)(2,1)S(1)}, u32[]{:S(2)}, u32[]{:S(2)}) collective-permute-start(bf16[2,512,512]{2,1,0:T(8,128)(2,1)S(1)} %broadcast_select_fusion.1.f), channel_id=1, source_target_pairs={{0,1},{1,0},{2,3},{3,2},{4,5},{5,4},{6,7},{7,6},{8,9},{9,8},{10,11... | collective-permute-start | bytes 3145736 | tf_op jit(solution)/shard_map/ppermute | solution.py:21
  95.3 29.8 %collective-permute-start.8 = (bf16[2,512,256]{2,1,0:T(8,128)(2,1)}, bf16[2,512,256]{2,1,0:T(8,128)(2,1)}, u32[]{:S(2)}, u32[]{:S(2)}) collective-permute-start(bf16[2,512,256]{2,1,0:T(8,128)(2,1)} %slice.18), channel_id=1, source_target_pairs={{2,0},{6,4},{10,8},{14,12},{18,16},{22,20},{26,24},{30,28},{3,1},{... | collective-permute-start | bytes 1572872 | tf_op jit(solution)/shard_map/ppermute | solution.py:17
  119.5 1.0 copy-start.2
